TPU v7x, 512 devices: a whole 4x4x16 slice. The times are simulated.
512 devices in a mesh: dp: 64 (over z, y_hi, core), tensor: 8 (over x, y_lo).
Axes of the slice: x: 4, y: 4 (y_hi: 2, y_lo: 2; y = y_hi * 2 + y_lo), z: 16, core: 2. Of those that a mesh axis runs over, the one named last changes fastest.
Arguments:
- context: bfloat16 [8192, 4096], P('dp', 'tensor'), may hold values from -6 to 6
- out_weight: bfloat16 [4096, 2048], P('tensor'), may hold values from -0.09375 to 0.09375
- residual_in: float32 [8192, 2048], P('dp', 'tensor')
- norm_gain: float32 [2048], P('tensor'), may hold values from 0.1 to 1.9
- expert_ids: int32 [8192, 8], P('dp'), may hold values from 0 to 63, all different within a row; in each aligned block of 128 rows (0 to 127, 128 to 255, ...) at most 24 rows name the same one
- expert_gates: float32 [8192, 8], P('dp'), may hold values from 0.05 to 1
- w_gate: bfloat16 [64, 1536, 2048], P('dp', 'tensor'), may hold values from -0.125 to 0.125
- w_up: bfloat16 [64, 1536, 2048], P('dp', 'tensor'), may hold values from -0.125 to 0.125
- w_down: bfloat16 [64, 1536, 2048], P('dp', None, 'tensor'), may hold values from -0.15625 to 0.15625
Outputs:
- attended: float32 [8192, 2048], P('dp', 'tensor')
- expert_mix: bfloat16 [8192, 2048], P('dp', 'tensor')
Inputs may be any that keep to these rules, and one draw needn't show every extreme that they name: `expert_ids`: each token names 8 different experts. The 128 tokens of one index of dp (aligned blocks of rows) name any one expert at most 24 times, a bound that some block reaches.
All inputs are finite; a program needn't handle non-finite values.
Results may differ from a plain program's by a relative error of at most 0.0071.
Values may be sent and summed in bfloat16 or wider, within the bound.
A program may use at most 64 MiB of HBM per device.

v0:
```python
import jax
import jax.numpy as jnp
from jax import lax
from jax.sharding import PartitionSpec as P

epsilon = 1e-06


def local(
    context, out_weight, residual_in, norm_gain, expert_ids, expert_gates, w_gate, w_up, w_down
):
    num_tokens, width_local = residual_in.shape
    summed_proj = lax.psum_scatter(
        jnp.einsum("th,hd->dt", context, out_weight, preferred_element_type=jnp.float32),
        "tensor",
        scatter_dimension=0,
        tiled=True,
    )
    attended = residual_in + summed_proj.T
    squares = lax.psum(jnp.sum(attended * attended, axis=1), "tensor")
    full_width = width_local * lax.axis_size("tensor")
    scaling = lax.rsqrt(squares / full_width + epsilon)
    normed = (attended * scaling[:, None] * norm_gain).astype(jnp.bfloat16)
    top_count = expert_ids.shape[1]
    num_experts = w_gate.shape[0] * lax.axis_size("dp")
    capacity = max(2, 3 * num_tokens * top_count // (2 * num_experts))
    flat_ids = expert_ids.reshape(-1)
    one_hot = (flat_ids[:, None] == jnp.arange(num_experts, dtype=jnp.int32)[None, :]).astype(
        jnp.int32
    )
    earlier = jnp.cumsum(one_hot, axis=0) - one_hot
    position = jnp.sum(earlier * one_hot, axis=1)
    slot_index = flat_ids * capacity + position
    pair_token = jnp.arange(num_tokens * top_count, dtype=jnp.int32) // top_count
    source_token = (
        jnp.full((num_experts * capacity,), num_tokens, jnp.int32).at[slot_index].set(pair_token)
    )
    gate_local = w_gate[0]
    up_local = w_up[0]
    down_local = w_down[0]
    full_rows = lax.all_gather(normed, "tensor", axis=1, tiled=True)
    padded_rows = jnp.concatenate(
        [full_rows, jnp.zeros((1, full_rows.shape[1]), jnp.bfloat16)], axis=0
    )
    outgoing = padded_rows[source_token].reshape(num_experts, capacity, full_rows.shape[1])
    received = lax.all_to_all(outgoing, "dp", split_axis=0, concat_axis=0, tiled=True)
    gate_val = jnp.einsum("scd,hd->sch", received, gate_local, preferred_element_type=jnp.float32)
    up_val = jnp.einsum("scd,hd->sch", received, up_local, preferred_element_type=jnp.float32)
    activation = (jax.nn.silu(gate_val) * up_val).astype(jnp.bfloat16)
    summed_out = jnp.einsum(
        "sch,hd->scd",
        lax.all_gather(activation, "tensor", axis=2, tiled=True),
        down_local,
        preferred_element_type=jnp.float32,
    )
    result = summed_out.astype(jnp.bfloat16)
    returned = lax.all_to_all(result, "dp", split_axis=0, concat_axis=0, tiled=True)
    flat_back = returned.reshape(num_experts * capacity, width_local)
    picked = flat_back[slot_index].reshape(num_tokens, top_count, width_local).astype(jnp.float32)
    weights = expert_gates / jnp.sum(expert_gates, axis=1, keepdims=True)
    expert_mix = jnp.sum(weights[:, :, None] * picked, axis=1).astype(jnp.bfloat16)
    return (attended, expert_mix)


def solution(mesh):
    return jax.shard_map(
        local,
        mesh=mesh,
        in_specs=(
            P("dp", "tensor"),
            P("tensor", None),
            P("dp", "tensor"),
            P("tensor"),
            P("dp", None),
            P("dp", None),
            P("dp", "tensor", None),
            P("dp", "tensor", None),
            P("dp", None, "tensor"),
        ),
        out_specs=(P("dp", "tensor"), P("dp", "tensor")),
        check_vma=False,
    )
```

profile of v0, /device:TPU:1, one launch (start us, length us, event | category | flops | bytes accessed | tf_op | source)
XLA Modules:
  0.0 695.6 jit_solution(4294117381571597590)
XLA Ops:
  7.2 1.5 copy-done
  8.8 2.6 fusion.14
  11.8 18.0 %reduce-window.6 = s32[64,8,128]{2,1,0:T(8,128)S(1)} reduce-window(s32[64,8,128]{2,1,0:T(8,128)S(1)} %fusion.8, s32[]{:T(128)} %constant.37.clone.1), window={size=1x1x128 pad=0_0x0_0x127_0}, to_apply=%region_4.5 | reduce-window | flops 8323072 | bytes 524292 | tf_op jit(solution)/shard_map/reduce-window
  29.9 0.1 copy.29
  30.8 4.3 scatter_custom_fusion
  35.1 24.9 %reduce-scatter.2.cloned.1.call-done = f32[256,128]{1,0:T(8,128)} async-done(((f32[2048,128]{1,0:T(8,128)}), f32[256,128]{1,0:T(8,128)}) %reduce-scatter.2.cloned.1.call-update) | async-done | bytes 131088 | tf_op jit(solution)/shard_map/reduce_scatter | solution.py:13
  60.0 1.0 multiply_reduce_fusion
  61.0 14.4 %psum.7 = f32[128]{0:T(128)S(1)} all-reduce(f32[128]{0:T(128)S(1)} %get-tuple-element.8), channel_id=1, replica_groups=mesh['dp'=64,'tensor'=8] {'tensor'}, use_global_device_ids=true, to_apply=%region_3.0 | all-reduce | flops 128 | bytes 1024 | tf_op jit(solution)/shard_map/psum | solution.py:20
  75.5 23.1 %all_gather.6 = bf16[128,2048]{0,1:T(8,128)(2,1)S(1)} all-gather(bf16[128,256]{0,1:T(8,128)(2,1)S(1)} %multiply_convert_fusion.1), channel_id=1, replica_groups=mesh['dp'=64,'tensor'=8] {'tensor'}, dimensions={1}, use_global_device_ids=true | all-gather | bytes 589824 | tf_op jit(solution)/shard_map/all_gather | solution.py:41
  98.5 0.2 copy.35
  98.8 7.1 %gather_fusion = bf16[1536,2048]{1,0:T(8,128)(2,1)} fusion(bf16[129,2048]{1,0:T(8,128)(2,1)S(1)} %concatenate.3.clone, s32[2048]{0:T(1024)S(1)} %pad_clamp_fusion), kind=kCustom, calls=%fused_computation | custom fusion | bytes 12589056 | tf_op jit(solution)/shard_map/gather | solution.py:45
  105.9 307.8 %all_to_all.10 = bf16[64,24,2048]{2,1,0:T(8,128)(2,1)S(1)} all-to-all(bf16[64,24,2048]{2,1,0:T(8,128)(2,1)} %bitcast.46), channel_id=1, replica_groups=mesh['dp'=64,'tensor'=8] {'dp'}, dimensions={0} | all-to-all | bytes 12582912 | tf_op jit(solution)/shard_map/all_to_all | solution.py:46
  413.7 2.1 fusion.3
  415.8 2.3 multiply_convert_fusion
  418.1 1.8 copy.32
  419.9 186.7 %all-gather.2.cloned.1.call-done = bf16[64,24,1536]{0,1,2:T(8,128)(2,1)} async-done(((bf16[64,24,192]{0,1,2:T(8,128)(2,1)}), bf16[64,24,1536]{0,1,2:T(8,128)(2,1)}) %all-gather.2.cloned.1.call-update) | async-done | bytes 4718608 | tf_op jit(solution)/shard_map/all_gather | solution.py:52
  606.6 13.3 %copy.33 = bf16[64,24,1536]{2,1,0:T(8,128)(2,1)} copy(bf16[64,24,1536]{0,1,2:T(8,128)(2,1)} %all-gather.2.cloned.1.call-done) | data formatting | bytes 9437184 | tf_op jit(solution)/shard_map/all_gather | solution.py:52
  619.9 4.6 convolution_convert_fusion
  624.5 15.7 %all-to-all-start.1 = ((bf16[64,24,256]{2,1,0:T(8,128)(2,1)}), bf16[64,24,256]{2,1,0:T(8,128)(2,1)S(1)}, u32[]{:S(2)}, u32[]{:S(2)}) async-start(bf16[64,24,256]{2,1,0:T(8,128)(2,1)} %convolution_convert_fusion), calls=%async_computation.2 | async-start | bytes 1572864 | tf_op jit(solution)/shard_map/all_to_all | solution.py:57
  640.3 0.7 copy.25
  641.1 0.8 copy.34
  641.8 42.0 %all-to-all-done.1 = bf16[64,24,256]{2,1,0:T(8,128)(2,1)S(1)} async-done(((bf16[64,24,256]{2,1,0:T(8,128)(2,1)}), bf16[64,24,256]{2,1,0:T(8,128)(2,1)S(1)}, u32[]{:S(2)}, u32[]{:S(2)}) %all-to-all-start.1) | async-done | bytes 786464 | tf_op jit(solution)/shard_map/all_to_all | solution.py:57
  683.8 3.9 gather_fusion.1
  687.7 1.0 fusion
  (45 shorter events, 1.4 us)
Async XLA Ops:
  7.2 1.6 copy-start
  7.2 4.3 copy-start.3
  7.2 52.8 %reduce-scatter.2.cloned.1.call-start = ((), (), s32[]{:S(2)}) async-start(), calls=%async_computation.3 | async-start | bytes 1179648 | tf_op jit(solution)/shard_map/reduce_scatter | solution.py:13
  11.4 19.0 %copy-start.2 = (f32[128,256]{1,0:T(8,128)S(1)}, f32[128,256]{1,0:T(8,128)}, u32[]{:S(2)}) copy-start(f32[128,256]{1,0:T(8,128)} %param.11) | copy-start | bytes 393220
  11.4 64.0 %copy-start.5 = (f32[256]{0:T(256)S(1)}, f32[256]{0:T(256)}, u32[]{:S(2)}) copy-start(f32[256]{0:T(256)} %param.12) | copy-start | bytes 3076
  11.4 595.1 %all-gather.2.cloned.1.call-start = ((), (), s32[]{:S(2)}) async-start(), calls=%async_computation.4 | async-start | bytes 10616832 | tf_op jit(solution)/shard_map/all_gather | solution.py:52
  105.9 307.8 %copy-start.6 = (bf16[1,192,2048]{2,1,0:T(8,128)(2,1)S(1)}, bf16[1,192,2048]{2,1,0:T(8,128)(2,1)}, u32[]{:S(2)}) copy-start(bf16[1,192,2048]{2,1,0:T(8,128)(2,1)} %param.15) | copy-start | bytes 2359300
  413.7 2.1 copy-start.7
  419.9 200.0 %copy-start.8 = (bf16[1,1536,256]{2,1,0:T(8,128)(2,1)S(1)}, bf16[1,1536,256]{2,1,0:T(8,128)(2,1)}, u32[]{:S(2)}) copy-start(bf16[1,1536,256]{2,1,0:T(8,128)(2,1)} %param.17) | copy-start | bytes 2359300
  619.9 20.4 %copy-start.4 = (f32[128,8]{0,1:T(8,128)S(1)}, f32[128,8]{0,1:T(8,128)}, u32[]{:S(2)}) copy-start(f32[128,8]{0,1:T(8,128)} %param.14) | copy-start | bytes 12292
  624.5 59.2 %all-to-all-start.1 = ((bf16[64,24,256]{2,1,0:T(8,128)(2,1)}), bf16[64,24,256]{2,1,0:T(8,128)(2,1)S(1)}, u32[]{:S(2)}, u32[]{:S(2)}) async-start(bf16[64,24,256]{2,1,0:T(8,128)(2,1)} %convolution_convert_fusion), calls=%async_computation.2 | async-start | bytes 1572864 | tf_op jit(solution)/shard_map/all_to_all | solution.py:57
  683.8 3.9 copy-start.1
Sparse Core Ops, SparseCore 0:
  11.5 48.4 reduce-scatter.1
  420.0 186.5 all-gather.1
where the time goes:
time: 701 us; the launch traced here: 696 us
  blocking collectives  345 us (49%)
  waiting for transfers between devices  254 us (36%)
  local copies, waits for them, and re-layouts  34.7 us (5%)
  other arithmetic  20.4 us (3%)
  starting transfers between devices  15.8 us (2%)
  between operations  14.3 us (2%)
  matrix products  11.6 us (2%)
    all_to_all x1, blocking collectives, local(): lax.all_to_all(outgoing, 'dp', split_axis=0, concat_axis=0, tiled=True)  308 us
    all_gather x1, waiting for transfers between devices, local(): lax.all_gather(activation, 'tensor', axis=2, tiled=True)  187 us
    all_to_all x1, waiting for transfers between devices, local(): lax.all_to_all(result, 'dp', split_axis=0, concat_axis=0, tiled=True)  42 us
    reduce_scatter x1, waiting for transfers between devices, local(): lax.psum_scatter(jnp.einsum('th,hd->dt', context, out_weight, preferred_e...  24.9 us
    all_gather x1, blocking collectives, local(): full_rows = lax.all_gather(normed, 'tensor', axis=1, tiled=True)  23.1 us
    another operation x3, other arithmetic  18.2 us
    all_to_all x1, starting transfers between devices, local(): lax.all_to_all(result, 'dp', split_axis=0, concat_axis=0, tiled=True)  15.7 us
    psum x1, blocking collectives, local(): squares = lax.psum(jnp.sum(attended * attended, axis=1), 'tensor')  14.4 us
  transfers between devices with their start and end apart: 3, of which 3 were waited for; matrix products, arithmetic and copies ran while one was open for 4% of the time, Pallas kernels for 0%

commit v1 on v0

v1 whole, which is shorter than its diff:
```python
import functools

import jax
import jax.numpy as jnp
from jax import lax
from jax.experimental import pallas as pl
from jax.experimental.pallas import tpu as pltpu
from jax.sharding import PartitionSpec as P

epsilon = 1e-06
MESH = pl.DeviceIdType.MESH
NX, NY = 4, 2
CHUNKS = 4


def neighbours():
    me = lax.axis_index("tensor")
    x, y = me // NY, lax.rem(me, NY)
    at = lambda dx, dy: lax.rem(x + dx, NX) * NY + lax.rem(y + dy, NY)
    owners = [me, at(0, 1), at(3, 0), at(1, 0), at(2, 0), at(3, 1), at(1, 1), at(2, 1)]
    return owners, at(0, 1), at(1, 0), at(3, 0)


class Gather:
    def __init__(self, own, view, sends, recvs, partner, right, left):
        kinds = [
            (own, view(1, None), partner),
            (own, view(2, None), right),
            (own, view(3, None), left),
            (view(2, 0), view(4, 0), right),
            (view(3, 1), view(4, 1), left),
            (view(1, None), view(5, None), right),
            (view(1, None), view(6, None), left),
            (view(4, None), view(7, None), partner),
        ]
        self.copies = [
            pltpu.make_async_remote_copy(
                src_ref=src, dst_ref=dst, send_sem=sends.at[k], recv_sem=recvs.at[k],
                device_id={"tensor": to}, device_id_type=MESH,
            )
            for k, (src, dst, to) in enumerate(kinds)
        ]

    def start(self):
        for k in (1, 2, 0):
            self.copies[k].start()

    def relay(self):
        c = self.copies
        c[1].wait_recv()
        c[3].start()
        c[2].wait_recv()
        c[4].start()
        c[0].wait_recv()
        c[5].start()
        c[6].start()

    def cross(self):
        c = self.copies
        c[3].wait_recv()
        c[4].wait_recv()
        c[7].start()

    def arrive(self):
        for k in (5, 6, 7):
            self.copies[k].wait_recv()

    def drain(self):
        for c in self.copies:
            c.wait_send()


def expert_kernel(
    x_ref, gate_ref, up_ref, down_ref, out_ref,
    xg, ag, wcat, wd1, wd2, own_sem, x_send, x_recv, a_send, a_recv,
):
    rows, width = x_ref.shape
    hidden = gate_ref.shape[0]
    rest = hidden - 128
    size = rows // CHUNKS
    packed = size + size // 2
    owners, partner, right, left = neighbours()

    barrier = pltpu.get_barrier_semaphore()
    for other in (partner, right, left):
        pl.semaphore_signal(barrier, inc=1, device_id={"tensor": other}, device_id_type=MESH)
    pl.semaphore_wait(barrier, 3)

    def x_view(c):
        def view(slot, half):
            start, count = c * size, size
            if half is not None:
                start, count = start + half * (size // 2), size // 2
            return xg.at[pl.ds(start, count), pl.ds(slot * width, width)]
        return view

    def a_view(c):
        def view(slot, half):
            start, count = c * packed, packed
            if half is not None:
                start, count = start + half * (packed // 2), packed // 2
            return ag.at[pl.ds(start, count), pl.ds(slot * 128, 128)]
        return view

    gx = [
        Gather(x_ref.at[pl.ds(c * size, size)], x_view(c), x_send.at[c], x_recv.at[c], partner, right, left)
        for c in range(CHUNKS)
    ]
    ga = [
        Gather(a_view(c)(0, None), a_view(c), a_send.at[c], a_recv.at[c], partner, right, left)
        for c in range(CHUNKS)
    ]
    for g in gx:
        g.start()
    own = pltpu.make_async_copy(x_ref, xg.at[:, pl.ds(0, width)], own_sem)
    own.start()

    wcat[...] = jnp.zeros_like(wcat)
    wd2[...] = jnp.zeros_like(wd2)
    for slot, owner in enumerate(owners):
        cols = pl.ds(pl.multiple_of(owner * width, width), width)
        here = pl.ds(slot * width, width)
        wcat[0:hidden, here] = gate_ref[:, cols]
        wcat[256:256 + hidden, here] = up_ref[:, cols]
        base = owner * hidden
        wd1[pl.ds(slot * 128, 128), :] = down_ref[pl.ds(pl.multiple_of(base, 64), 128), :]
        tail = down_ref[pl.ds(pl.multiple_of(base + 128, 64), rest), :]
        wd2[pl.ds(slot * 128, rest), 0:width] = tail
        wd2[pl.ds(slot * 128 + rest, rest), width:2 * width] = tail
    own.wait()

    def gate_up(c):
        h = lax.dot_general(
            xg[pl.ds(c * size, size), :], wcat[...], (((1,), (1,)), ((), ())),
            preferred_element_type=jnp.float32,
        )
        gate, up = h[:, 0:256], h[:, 256:512]
        act = gate / (1.0 + jnp.exp(-gate)) * up
        tail = act[:, 128:256]
        tail = tail[0:size // 2] + pltpu.roll(tail[size // 2:size], 64, 1)
        ag[pl.ds(c * packed, size), 0:128] = act[:, 0:128].astype(jnp.bfloat16)
        ag[pl.ds(c * packed + size, size // 2), 0:128] = tail.astype(jnp.bfloat16)

    def down(c):
        first = jnp.dot(ag[pl.ds(c * packed, size), :], wd1[...], preferred_element_type=jnp.float32)
        second = jnp.dot(
            ag[pl.ds(c * packed + size, size // 2), :], wd2[...], preferred_element_type=jnp.float32
        )
        half = size // 2
        out_ref[pl.ds(c * size, half), :] = (first[0:half] + second[:, 0:width]).astype(jnp.bfloat16)
        out_ref[pl.ds(c * size + half, half), :] = (first[half:] + second[:, width:]).astype(jnp.bfloat16)

    for step in range(CHUNKS + 5):
        at = lambda lag: step - lag if 0 <= step - lag < CHUNKS else None
        if at(0) is not None:
            gx[at(0)].relay()
        if at(1) is not None:
            gx[at(1)].cross()
        if at(2) is not None:
            gx[at(2)].arrive()
            gate_up(at(2))
            ga[at(2)].start()
        if at(3) is not None:
            ga[at(3)].relay()
        if at(4) is not None:
            ga[at(4)].cross()
        if at(5) is not None:
            ga[at(5)].arrive()
            down(at(5))
    for g in gx + ga:
        g.drain()


def experts(x, gate, up, down):
    rows, width = x.shape
    size = rows // CHUNKS
    packed = size + size // 2
    vmem = pl.BlockSpec(memory_space=pltpu.VMEM)
    return pl.pallas_call(
        expert_kernel,
        out_shape=jax.ShapeDtypeStruct((rows, width), jnp.bfloat16),
        in_specs=[vmem] * 4,
        out_specs=vmem,
        scratch_shapes=[
            pltpu.VMEM((rows, 8 * width), jnp.bfloat16),
            pltpu.VMEM((CHUNKS * packed, 8 * 128), jnp.bfloat16),
            pltpu.VMEM((512, 8 * width), jnp.bfloat16),
            pltpu.VMEM((8 * 128, width), jnp.bfloat16),
            pltpu.VMEM((8 * 128, 2 * width), jnp.bfloat16),
            pltpu.SemaphoreType.DMA,
            pltpu.SemaphoreType.DMA((CHUNKS, 8)),
            pltpu.SemaphoreType.DMA((CHUNKS, 8)),
            pltpu.SemaphoreType.DMA((CHUNKS, 8)),
            pltpu.SemaphoreType.DMA((CHUNKS, 8)),
        ],
        compiler_params=pltpu.CompilerParams(
            collective_id=0, has_side_effects=True, vmem_limit_bytes=48 * 1024 * 1024
        ),
    )(x, gate, up, down)


def local(
    context, out_weight, residual_in, norm_gain, expert_ids, expert_gates, w_gate, w_up, w_down
):
    num_tokens, width_local = residual_in.shape
    top_count = expert_ids.shape[1]
    num_experts = w_gate.shape[0] * lax.axis_size("dp")
    capacity = max(2, 3 * num_tokens * top_count // (2 * num_experts))
    slots = num_experts * capacity
    summed_proj = lax.psum_scatter(
        jnp.einsum("th,hd->dt", context, out_weight, preferred_element_type=jnp.float32),
        "tensor",
        scatter_dimension=0,
        tiled=True,
    )
    weights = expert_gates / jnp.sum(expert_gates, axis=1, keepdims=True)
    named = expert_ids[:, :, None] == jnp.arange(num_experts, dtype=jnp.int32)[None, None, :]
    member = jnp.any(named, axis=1)
    weight = jnp.sum(jnp.where(named, weights[:, :, None], 0.0), axis=1)
    order = jnp.arange(num_tokens, dtype=jnp.int32)
    before = (order[None, :] < order[:, None]).astype(jnp.bfloat16)
    rank = jnp.dot(before, member.astype(jnp.bfloat16), preferred_element_type=jnp.float32)
    rank = jnp.where(member, rank, -1.0).astype(jnp.bfloat16)
    slot = jnp.arange(slots, dtype=jnp.int32)
    spread = (slot[None, :] // capacity == jnp.arange(num_experts, dtype=jnp.int32)[:, None]).astype(
        jnp.bfloat16
    )
    high = lax.reduce_precision(weight, 8, 7)
    low = weight - high
    stacked = jnp.concatenate([rank, high.astype(jnp.bfloat16), low.astype(jnp.bfloat16)], axis=0)
    wide = jnp.dot(stacked, spread, preferred_element_type=jnp.float32)
    place = wide[:num_tokens] == (slot % capacity).astype(jnp.float32)[None, :]
    mix_high = jnp.where(place, wide[num_tokens:2 * num_tokens], 0.0).astype(jnp.bfloat16)
    mix_low = jnp.where(place, wide[2 * num_tokens:], 0.0).astype(jnp.bfloat16)
    place = place.astype(jnp.bfloat16)

    attended = residual_in + summed_proj.T
    squares = lax.psum(jnp.sum(attended * attended, axis=1), "tensor")
    full_width = width_local * lax.axis_size("tensor")
    scaling = lax.rsqrt(squares / full_width + epsilon)
    normed = (attended * scaling[:, None] * norm_gain).astype(jnp.bfloat16)

    outgoing = lax.dot_general(
        place, normed, (((0,), (0,)), ((), ())), preferred_element_type=jnp.float32
    ).astype(jnp.bfloat16)
    outgoing = outgoing.reshape(num_experts, capacity, width_local)
    received = lax.all_to_all(outgoing, "dp", split_axis=0, concat_axis=0, tiled=True)
    result = experts(received.reshape(slots, width_local), w_gate[0], w_up[0], w_down[0])
    result = result.reshape(num_experts, capacity, width_local)
    returned = lax.all_to_all(result, "dp", split_axis=0, concat_axis=0, tiled=True)
    flat_back = returned.reshape(slots, width_local)
    mixed = jnp.dot(mix_high, flat_back, preferred_element_type=jnp.float32)
    mixed = mixed + jnp.dot(mix_low, flat_back, preferred_element_type=jnp.float32)
    return (attended, mixed.astype(jnp.bfloat16))


def solution(mesh):
    return jax.shard_map(
        local,
        mesh=mesh,
        in_specs=(
            P("dp", "tensor"),
            P("tensor", None),
            P("dp", "tensor"),
            P("tensor"),
            P("dp", None),
            P("dp", None),
            P("dp", "tensor", None),
            P("dp", "tensor", None),
            P("dp", None, "tensor"),
        ),
        out_specs=(P("dp", "tensor"), P("dp", "tensor")),
        check_vma=False,
    )
```

time: 701 us -> 287 us (0.41)
  blocking collectives: 345 us -> 81.2 us
  waiting for transfers between devices: 254 us -> 88.6 us
  Pallas kernels: 0 us -> 79.5 us
  local copies, waits for them, and re-layouts: 34.7 us -> 3.8 us
  other arithmetic: 20.4 us -> 1.2 us
    all_to_all x1, blocking collectives: 308 us -> 66.8 us  [local(): lax.all_to_all(outgoing, 'dp', split_axis=0, concat_axis=0, tiled=True)]
    all_gather x1 -> x0, waiting for transfers between devices: 187 us -> none  [local(): lax.all_gather(activation, 'tensor', axis=2, tiled=True)]
    pallas_call x0 -> x1, Pallas kernels: none -> 79.5 us  [experts(): pl.pallas_call(expert_kernel, out_shape=jax.ShapeDtypeStruct((rows, width...]
    all_gather x1 -> x0, blocking collectives: 23.1 us -> none  [local(): full_rows = lax.all_gather(normed, 'tensor', axis=1, tiled=True)]
    reduce_scatter x1, waiting for transfers between devices: 24.9 us -> 45.9 us  [local(): lax.psum_scatter(jnp.einsum('th,hd->dt', context, out_weight, preferred_e...]
    another operation x3 -> x0, other arithmetic: 18.2 us -> none
    all_gather x1 -> x0, local copies, waits for them, and re-layouts: 13.3 us -> none  [local(): lax.all_gather(activation, 'tensor', axis=2, tiled=True)]
    gather x2 -> x0, local copies, waits for them, and re-layouts: 11 us -> none  [the longest x1 7.09 us: local(): padded_rows[source_token].reshape(num_experts, capacity, full_rows.shape[1])]
  transfers between devices with their start and end apart: 3 -> 2, of which waited for: 3 -> 2; matrix products, arithmetic and copies ran while one was open for 4% -> 1% of each run, Pallas kernels for 0% -> 0%
where the time goes in v1:
time: 287 us; the launch traced here: 286 us
  waiting for transfers between devices  88.6 us (31%)
  blocking collectives  81.2 us (28%)
  Pallas kernels  79.5 us (28%)
  between operations  14.2 us (5%)
  starting transfers between devices  9.95 us (3%)
  matrix products  7.14 us (2%)
  local copies, waits for them, and re-layouts  3.8 us (1%)
    pallas_call x1, Pallas kernels, experts(): pl.pallas_call(expert_kernel, out_shape=jax.ShapeDtypeStruct((rows, width...  79.5 us
    all_to_all x1, blocking collectives, local(): lax.all_to_all(outgoing, 'dp', split_axis=0, concat_axis=0, tiled=True)  66.8 us
    reduce_scatter x1, waiting for transfers between devices, local(): lax.psum_scatter(jnp.einsum('th,hd->dt', context, out_weight, preferred_e...  45.9 us
    all_to_all x1, waiting for transfers between devices, local(): lax.all_to_all(result, 'dp', split_axis=0, concat_axis=0, tiled=True)  42.7 us
    psum x1, blocking collectives, local(): squares = lax.psum(jnp.sum(attended * attended, axis=1), 'tensor')  14.4 us
    all_to_all x1, starting transfers between devices, local(): lax.all_to_all(result, 'dp', split_axis=0, concat_axis=0, tiled=True)  9.91 us
  transfers between devices with their start and end apart: 2, of which 2 were waited for; matrix products, arithmetic and copies ran while one was open for 1% of the time, Pallas kernels for 0%

profile of v1, /device:TPU:1, one launch (start us, length us, event | category | flops | bytes accessed | tf_op | source)
XLA Modules:
  0.0 285.7 jit_solution(758459261116152694)
XLA Ops:
  7.2 0.0 copy-start
  7.2 0.0 copy-start.5
  7.2 0.0 reduce-scatter.2.cloned.1.call-start
  7.3 1.5 copy-done
  8.8 2.6 fusion.32
  11.4 0.0 reduce-scatter.2.cloned.1.call-update
  11.4 0.0 copy-start.8
  11.4 0.1 copy.15
  11.7 0.1 fusion.1
  11.9 0.5 fusion.10
  12.4 1.4 copy-done.4
  13.8 0.1 slice_compare_fusion
  13.9 45.9 %reduce-scatter.2.cloned.1.call-done = f32[256,128]{1,0:T(8,128)} async-done(((f32[2048,128]{1,0:T(8,128)}), f32[256,128]{1,0:T(8,128)}) %reduce-scatter.2.cloned.1.call-update) | async-done | bytes 131088 | tf_op jit(solution)/shard_map/reduce_scatter | solution.py:210
  59.8 1.0 multiply_reduce_fusion
  60.7 14.4 %psum.7 = f32[128]{0:T(128)S(1)} all-reduce(f32[128]{0:T(128)S(1)} %get-tuple-element.6), channel_id=1, replica_groups=mesh['dp'=64,'tensor'=8] {'tensor'}, use_global_device_ids=true, to_apply=%region_5.6 | all-reduce | flops 128 | bytes 1024 | tf_op jit(solution)/shard_map/psum | solution.py:238
  75.2 0.5 convolution_convert_fusion
  75.6 66.8 %all_to_all.10 = bf16[64,24,256]{2,1,0:T(8,128)(2,1)S(1)} all-to-all(bf16[64,24,256]{2,1,0:T(8,128)(2,1)S(1)} %bitcast.21), channel_id=1, replica_groups=mesh['dp'=64,'tensor'=8] {'dp'}, dimensions={0} | all-to-all | bytes 1572864 | tf_op jit(solution)/shard_map/all_to_all | solution.py:247
  142.4 0.0 copy-done.1
  142.4 79.5 %shard_map.104 = bf16[1536,256]{1,0:T(8,128)(2,1)} custom-call(bf16[1536,256]{1,0:T(8,128)(2,1)S(1)} %bitcast.15, bf16[192,2048]{1,0:T(8,128)(2,1)S(1)} %bitcast.16, bf16[192,2048]{1,0:T(8,128)(2,1)S(1)} %bitcast.17, bf16[1536,256]{1,0:T(8,128)(2,1)S(1)} %bitcast.18), custom_call_target="tpu_custom_call" | custom-call | tf_op jit(solution)/shard_map/pallas_call | solution.py:179
  222.0 9.9 %all-to-all-start.1 = ((bf16[64,24,256]{2,1,0:T(8,128)(2,1)}), bf16[64,24,256]{2,1,0:T(8,128)(2,1)S(1)}, u32[]{:S(2)}, u32[]{:S(2)}) async-start(bf16[64,24,256]{2,1,0:T(8,128)(2,1)} %bitcast.6), calls=%async_computation.2 | async-start | bytes 1572864 | tf_op jit(solution)/shard_map/all_to_all | solution.py:250
  231.9 0.8 copy.16
  232.6 42.7 %all-to-all-done.1 = bf16[64,24,256]{2,1,0:T(8,128)(2,1)S(1)} async-done(((bf16[64,24,256]{2,1,0:T(8,128)(2,1)}), bf16[64,24,256]{2,1,0:T(8,128)(2,1)S(1)}, u32[]{:S(2)}, u32[]{:S(2)}) %all-to-all-start.1) | async-done | bytes 786464 | tf_op jit(solution)/shard_map/all_to_all | solution.py:250
  275.4 1.4 fusion.4
  276.8 2.0 fusion
  (20 shorter events, 0.2 us)
Async XLA Ops:
  7.2 1.6 copy-start
  7.2 4.2 %copy-start.5 = (f32[128,256]{1,0:T(8,128)S(1)}, f32[128,256]{1,0:T(8,128)}, u32[]{:S(2)}) copy-start(f32[128,256]{1,0:T(8,128)} %param.11) | copy-start | bytes 393220
  7.2 4.3 %copy-start.7 = (f32[128,8]{0,1:T(8,128)S(1)}, f32[128,8]{0,1:T(8,128)}, u32[]{:S(2)}) copy-start(f32[128,8]{0,1:T(8,128)} %param.14) | copy-start | bytes 12292
  7.2 4.4 %copy-start.6 = (s32[128,8]{0,1:T(8,128)S(1)}, s32[128,8]{0,1:T(8,128)}, u32[]{:S(2)}) copy-start(s32[128,8]{0,1:T(8,128)} %param.13) | copy-start | bytes 12292
  7.2 52.6 %reduce-scatter.2.cloned.1.call-start = ((), (), s32[]{:S(2)}) async-start(), calls=%async_computation.3 | async-start | bytes 1179648 | tf_op jit(solution)/shard_map/reduce_scatter | solution.py:210
  11.4 63.7 %copy-start.8 = (f32[256]{0:T(256)S(1)}, f32[256]{0:T(256)}, u32[]{:S(2)}) copy-start(f32[256]{0:T(256)} %param.12) | copy-start | bytes 3076
  12.3 1.4 copy-start.4
  13.8 128.6 %copy-start.1 = (bf16[1,192,2048]{2,1,0:T(8,128)(2,1)S(1)}, bf16[1,192,2048]{2,1,0:T(8,128)(2,1)}, u32[]{:S(2)}) copy-start(bf16[1,192,2048]{2,1,0:T(8,128)(2,1)} %param.15) | copy-start | bytes 2359300
  75.1 67.3 %copy-start.2 = (bf16[1,192,2048]{2,1,0:T(8,128)(2,1)S(1)}, bf16[1,192,2048]{2,1,0:T(8,128)(2,1)}, u32[]{:S(2)}) copy-start(bf16[1,192,2048]{2,1,0:T(8,128)(2,1)} %param.16) | copy-start | bytes 2359300
  75.1 67.3 %copy-start.3 = (bf16[1,1536,256]{2,1,0:T(8,128)(2,1)S(1)}, bf16[1,1536,256]{2,1,0:T(8,128)(2,1)}, u32[]{:S(2)}) copy-start(bf16[1,1536,256]{2,1,0:T(8,128)(2,1)} %param.17) | copy-start | bytes 2359300
  222.0 53.4 %all-to-all-start.1 = ((bf16[64,24,256]{2,1,0:T(8,128)(2,1)}), bf16[64,24,256]{2,1,0:T(8,128)(2,1)S(1)}, u32[]{:S(2)}, u32[]{:S(2)}) async-start(bf16[64,24,256]{2,1,0:T(8,128)(2,1)} %bitcast.6), calls=%async_computation.2 | async-start | bytes 1572864 | tf_op jit(solution)/shard_map/all_to_all | solution.py:250
Sparse Core Ops, SparseCore 0:
  11.5 48.2 reduce-scatter.1

commit v2 on v1

v2 whole, which is shorter than its diff:
```python
import functools

import jax
import jax.numpy as jnp
from jax import lax
from jax.experimental import pallas as pl
from jax.experimental.pallas import tpu as pltpu
from jax.sharding import PartitionSpec as P

epsilon = 1e-06
MESH = pl.DeviceIdType.MESH
NX, NY, NZ, DP = 4, 2, 16, 64
CHUNKS = 4


def neighbours():
    me = lax.axis_index("tensor")
    x, y = me // NY, lax.rem(me, NY)
    at = lambda dx, dy: lax.rem(x + dx, NX) * NY + lax.rem(y + dy, NY)
    owners = [me, at(0, 1), at(3, 0), at(1, 0), at(2, 0), at(3, 1), at(1, 1), at(2, 1)]
    return owners, at(0, 1), at(1, 0), at(3, 0)


class Gather:
    def __init__(self, own, view, sends, recvs, partner, right, left):
        kinds = [
            (own, view(1, None), partner),
            (own, view(2, None), right),
            (own, view(3, None), left),
            (view(2, 0), view(4, 0), right),
            (view(3, 1), view(4, 1), left),
            (view(1, None), view(5, None), right),
            (view(1, None), view(6, None), left),
            (view(4, None), view(7, None), partner),
        ]
        self.copies = [
            pltpu.make_async_remote_copy(
                src_ref=src, dst_ref=dst, send_sem=sends.at[k], recv_sem=recvs.at[k],
                device_id={"tensor": to}, device_id_type=MESH,
            )
            for k, (src, dst, to) in enumerate(kinds)
        ]

    def start(self):
        for k in (1, 2, 0):
            self.copies[k].start()

    def relay(self):
        c = self.copies
        c[1].wait_recv()
        c[3].start()
        c[2].wait_recv()
        c[4].start()
        c[0].wait_recv()
        c[5].start()
        c[6].start()

    def cross(self):
        c = self.copies
        c[3].wait_recv()
        c[4].wait_recv()
        c[7].start()

    def arrive(self):
        for k in (5, 6, 7):
            self.copies[k].wait_recv()

    def drain(self):
        for c in self.copies:
            c.wait_send()


def peer(p, sign):
    dp = lax.axis_index("dp")
    i, a, b = p // 4, lax.rem(p // 2, 2), lax.rem(p, 2)
    odd = lax.rem(i, 2)
    dz = odd * ((i + 1) // 2) + (1 - odd) * lax.rem(NZ - i // 2, NZ)
    z = lax.rem(dp // 4 + NZ + sign * dz, NZ)
    return z * 4 + lax.rem(lax.rem(dp // 2, 2) + a, 2) * 2 + lax.rem(lax.rem(dp, 2) + b, 2)


def expert_kernel(
    x_ref, high_ref, low_ref, gate_ref, up_ref, down_ref, out_ref,
    xg, ag, wlo, whi, wd1, wd2, ob, ret, own_sem, d_send, d_recv, r_send, r_recv,
    x_send, x_recv, a_send, a_recv,
):
    slots = x_ref.shape[0]
    block = slots // DP
    row = block // 2
    hidden = gate_ref.shape[0]
    rest = hidden - 128
    per = DP // CHUNKS
    xsize = per * block
    size = per * row
    packed = size + size // 2
    owners, partner, right, left = neighbours()
    me = lax.axis_index("dp")

    barrier = pltpu.get_barrier_semaphore()
    for other in (partner, right, left):
        pl.semaphore_signal(barrier, inc=1, device_id={"tensor": other}, device_id_type=MESH)

    @pl.loop(1, DP)
    def _(p):
        pl.semaphore_signal(barrier, inc=1, device_id={"dp": peer(p, 1)}, device_id_type=MESH)

    wlo[...] = jnp.zeros_like(wlo)
    whi[...] = jnp.zeros_like(whi)
    wd2[...] = jnp.zeros_like(wd2)
    for slot, owner in enumerate(owners):
        here = pl.ds(slot * 128, 128)
        for part, w in enumerate((wlo, whi)):
            cols = pl.ds(pl.multiple_of(owner * 256 + part * 128, 128), 128)
            w[0:hidden, here] = gate_ref[:, cols]
            w[256:256 + hidden, here] = up_ref[:, cols]
        base = owner * hidden
        wd1[here, :] = down_ref[pl.ds(pl.multiple_of(base, 64), 128), :]
        tail = down_ref[pl.ds(pl.multiple_of(base + 128, 64), rest), :]
        wd2[pl.ds(slot * 128, rest), 0:256] = tail
        wd2[pl.ds(slot * 128 + rest, rest), 256:512] = tail
    pl.semaphore_wait(barrier, 3 + DP - 1)

    def rows_at(p):
        return pl.ds(pl.multiple_of(p * block, 16), block)

    def send(p):
        to = peer(p, -1)
        return pltpu.make_async_remote_copy(
            src_ref=x_ref.at[rows_at(to)], dst_ref=xg.at[rows_at(p), pl.ds(0, 128)],
            send_sem=d_send, recv_sem=d_recv.at[p // per], device_id={"dp": to}, device_id_type=MESH,
        )

    def give_back(p):
        to = peer(p, 1)
        return pltpu.make_async_remote_copy(
            src_ref=ob.at[rows_at(p)], dst_ref=ret.at[rows_at(me)],
            send_sem=r_send, recv_sem=r_recv, device_id={"dp": to}, device_id_type=MESH,
        )

    @pl.loop(1, DP)
    def _(p):
        send(p).start()

    own = pltpu.make_async_copy(x_ref.at[rows_at(me)], xg.at[pl.ds(0, block), pl.ds(0, 128)], own_sem.at[0])
    own.start()
    own_back = pltpu.make_async_copy(ob.at[pl.ds(0, block)], ret.at[rows_at(me)], own_sem.at[1])

    def wait_for(ref, sem):
        pltpu.make_async_copy(ref, ref, sem).wait()

    def received(c):
        if c == 0:
            wait_for(xg.at[pl.ds(block, xsize - block), pl.ds(0, 128)], d_recv.at[0])
            own.wait()
        else:
            wait_for(xg.at[pl.ds(c * xsize, xsize), pl.ds(0, 128)], d_recv.at[c])

    def view_of(buf, rows, c):
        def view(slot, half):
            start, count = c * rows, rows
            if half is not None:
                start, count = start + half * (rows // 2), rows // 2
            return buf.at[pl.ds(start, count), pl.ds(slot * 128, 128)]
        return view

    def gathers(buf, rows, sends, recvs):
        views = [view_of(buf, rows, c) for c in range(CHUNKS)]
        return [
            Gather(v(0, None), v, sends.at[c], recvs.at[c], partner, right, left)
            for c, v in enumerate(views)
        ]

    gx = gathers(xg, xsize, x_send, x_recv)
    ga = gathers(ag, packed, a_send, a_recv)

    def times(x, w):
        h = lax.dot_general(x, w, (((1,), (1,)), ((), ())), preferred_element_type=jnp.float32)
        return h.reshape(per, block, 512)

    def gate_up(c):
        x = xg[pl.ds(c * xsize, xsize), :]
        h = times(x, wlo[...])[:, 0:row] + times(x, whi[...])[:, row:]
        h = h.reshape(size, 512)
        gate, up = h[:, 0:256], h[:, 256:512]
        act = gate / (1.0 + jnp.exp(-gate)) * up
        tail = act[:, 128:256]
        tail = tail[0:size // 2] + pltpu.roll(tail[size // 2:size], 64, 1)
        ag[pl.ds(c * packed, size), 0:128] = act[:, 0:128].astype(jnp.bfloat16)
        ag[pl.ds(c * packed + size, size // 2), 0:128] = tail.astype(jnp.bfloat16)

    def down(c):
        first = jnp.dot(ag[pl.ds(c * packed, size), :], wd1[...], preferred_element_type=jnp.float32)
        second = jnp.dot(
            ag[pl.ds(c * packed + size, size // 2), :], wd2[...], preferred_element_type=jnp.float32
        )
        second = jnp.concatenate([second[:, 0:256], second[:, 256:512]], axis=0)
        result = (first + second).reshape(per, row, 256)
        result = jnp.concatenate([result[:, :, 0:128], result[:, :, 128:256]], axis=1)
        ob[pl.ds(c * xsize, xsize), :] = result.reshape(xsize, 128).astype(jnp.bfloat16)
        if c == 0:
            own_back.start()

        @pl.loop(max(1, c * per), (c + 1) * per)
        def _(p):
            give_back(p).start()

    for step in range(CHUNKS + 6):
        at = lambda lag: step - lag if 0 <= step - lag < CHUNKS else None
        if at(0) is not None:
            received(at(0))
            gx[at(0)].start()
        if at(1) is not None:
            gx[at(1)].relay()
        if at(2) is not None:
            gx[at(2)].cross()
        if at(3) is not None:
            gx[at(3)].arrive()
            gate_up(at(3))
            ga[at(3)].start()
        if at(4) is not None:
            ga[at(4)].relay()
        if at(5) is not None:
            ga[at(5)].cross()
        if at(6) is not None:
            ga[at(6)].arrive()
            down(at(6))
    own_back.wait()
    others = pl.ds(0, slots - block)
    wait_for(ret.at[others], r_recv)

    back = ret[...]
    lower = lax.rem(lax.broadcasted_iota(jnp.int32, (slots, 128), 0), block) < row
    zero = jnp.zeros_like(back)
    back = jnp.concatenate([jnp.where(lower, back, zero), jnp.where(lower, zero, back)], axis=1)
    mixed = jnp.dot(high_ref[...], back, preferred_element_type=jnp.float32)
    mixed = mixed + jnp.dot(low_ref[...], back, preferred_element_type=jnp.float32)
    out_ref[...] = mixed.astype(jnp.bfloat16)

    wait_for(x_ref.at[others], d_send)
    wait_for(ob.at[others], r_send)
    for g in gx + ga:
        g.drain()


def experts(x, high, low, gate, up, down):
    slots = x.shape[0]
    packed = slots // 2 * 3 // 2
    vmem = pl.BlockSpec(memory_space=pltpu.VMEM)
    dma = pltpu.SemaphoreType.DMA
    return pl.pallas_call(
        expert_kernel,
        out_shape=jax.ShapeDtypeStruct((high.shape[0], 256), jnp.bfloat16),
        in_specs=[vmem] * 6,
        out_specs=vmem,
        scratch_shapes=[
            pltpu.VMEM((slots, 8 * 128), jnp.bfloat16),
            pltpu.VMEM((packed, 8 * 128), jnp.bfloat16),
            pltpu.VMEM((512, 8 * 128), jnp.bfloat16),
            pltpu.VMEM((512, 8 * 128), jnp.bfloat16),
            pltpu.VMEM((8 * 128, 256), jnp.bfloat16),
            pltpu.VMEM((8 * 128, 512), jnp.bfloat16),
            pltpu.VMEM((slots, 128), jnp.bfloat16),
            pltpu.VMEM((slots, 128), jnp.bfloat16),
            dma((2,)), dma, dma((CHUNKS,)), dma, dma,
            dma((CHUNKS, 8)), dma((CHUNKS, 8)), dma((CHUNKS, 8)), dma((CHUNKS, 8)),
        ],
        compiler_params=pltpu.CompilerParams(
            collective_id=0, has_side_effects=True, vmem_limit_bytes=56 * 1024 * 1024
        ),
    )(x, high, low, gate, up, down)


def local(
    context, out_weight, residual_in, norm_gain, expert_ids, expert_gates, w_gate, w_up, w_down
):
    num_tokens, width_local = residual_in.shape
    top_count = expert_ids.shape[1]
    num_experts = w_gate.shape[0] * lax.axis_size("dp")
    capacity = max(2, 3 * num_tokens * top_count // (2 * num_experts))
    summed_proj = lax.psum_scatter(
        jnp.einsum("th,hd->dt", context, out_weight, preferred_element_type=jnp.float32),
        "tensor",
        scatter_dimension=0,
        tiled=True,
    )
    weights = expert_gates / jnp.sum(expert_gates, axis=1, keepdims=True)
    named = expert_ids[:, :, None] == jnp.arange(num_experts, dtype=jnp.int32)[None, None, :]
    member = jnp.any(named, axis=1)
    weight = jnp.sum(jnp.where(named, weights[:, :, None], 0.0), axis=1)
    order = jnp.arange(num_tokens, dtype=jnp.int32)
    before = (order[None, :] < order[:, None]).astype(jnp.bfloat16)
    rank = jnp.dot(before, member.astype(jnp.bfloat16), preferred_element_type=jnp.float32)
    rank = jnp.where(member, rank, -1.0).astype(jnp.bfloat16)
    block = 2 * capacity
    slot = jnp.arange(num_experts * block, dtype=jnp.int32)
    spread = (slot[None, :] // block == jnp.arange(num_experts, dtype=jnp.int32)[:, None]).astype(
        jnp.bfloat16
    )
    high = lax.reduce_precision(weight, 8, 7)
    low = weight - high
    stacked = jnp.concatenate([rank, high.astype(jnp.bfloat16), low.astype(jnp.bfloat16)], axis=0)
    wide = jnp.dot(stacked, spread, preferred_element_type=jnp.float32)
    place = wide[:num_tokens] == (slot % capacity).astype(jnp.float32)[None, :]
    mix_high = jnp.where(place, wide[num_tokens:2 * num_tokens], 0.0).astype(jnp.bfloat16)
    mix_low = jnp.where(place, wide[2 * num_tokens:], 0.0).astype(jnp.bfloat16)
    place = place.astype(jnp.bfloat16)

    attended = residual_in + summed_proj.T
    squares = lax.psum(jnp.sum(attended * attended, axis=1), "tensor")
    full_width = width_local * lax.axis_size("tensor")
    scaling = lax.rsqrt(squares / full_width + epsilon)
    normed = (attended * scaling[:, None] * norm_gain).astype(jnp.bfloat16)

    outgoing = lax.dot_general(
        place, normed, (((0,), (0,)), ((), ())), preferred_element_type=jnp.float32
    )
    lower = (slot % block < capacity)[:, None]
    outgoing = jnp.where(lower, outgoing[:, :128], outgoing[:, 128:]).astype(jnp.bfloat16)
    mixed = experts(outgoing, mix_high, mix_low, w_gate[0], w_up[0], w_down[0])
    return (attended, mixed)


def solution(mesh):
    return jax.shard_map(
        local,
        mesh=mesh,
        in_specs=(
            P("dp", "tensor"),
            P("tensor", None),
            P("dp", "tensor"),
            P("tensor"),
            P("dp", None),
            P("dp", None),
            P("dp", "tensor", None),
            P("dp", "tensor", None),
            P("dp", None, "tensor"),
        ),
        out_specs=(P("dp", "tensor"), P("dp", "tensor")),
        check_vma=False,
    )
```

time: 287 us -> 240 us (0.84)
  Pallas kernels: 79.5 us -> 149 us
  blocking collectives: 81.2 us -> 14.6 us
  waiting for transfers between devices: 88.6 us -> 44.8 us
  starting transfers between devices: 9.95 us -> 0.04 us
  other arithmetic: 1.2 us -> 5.76 us
  matrix products: 7.14 us -> 4.24 us
    pallas_call x1, Pallas kernels: 79.5 us -> 149 us  [experts(): pl.pallas_call(expert_kernel, out_shape=jax.ShapeDtypeStruct((high.shape[...]
    all_to_all x1 -> x0, blocking collectives: 66.8 us -> none  [local(): lax.all_to_all(outgoing, 'dp', split_axis=0, concat_axis=0, tiled=True)]
    all_to_all x1 -> x0, waiting for transfers between devices: 42.7 us -> none  [local(): lax.all_to_all(result, 'dp', split_axis=0, concat_axis=0, tiled=True)]
    all_to_all x1 -> x0, starting transfers between devices: 9.91 us -> none  [local(): lax.all_to_all(result, 'dp', split_axis=0, concat_axis=0, tiled=True)]
    convert_element_type x0 -> x3, other arithmetic: none -> 4.65 us  [the longest x1 2.34 us: local(): jnp.where(lower, outgoing[:, :128], outgoing[:, 128:]).astype(jnp.bfloat16)]
    dot_general x2 -> x0, matrix products: 3.44 us -> none  [the longest x1 2.04 us: local(): jnp.dot(mix_low, flat_back, preferred_element_type=jnp.float32)]
  transfers between devices with their start and end apart: 2 -> 1, of which waited for: 2 -> 1; matrix products, arithmetic and copies ran while one was open for 1% -> 1% of each run, Pallas kernels for 0% -> 0%
where the time goes in v2:
time: 240 us; the launch traced here: 237 us
  Pallas kernels  149 us (62%)
  waiting for transfers between devices  44.8 us (19%)
  blocking collectives  14.6 us (6%)
  between operations  14.2 us (6%)
  other arithmetic  5.76 us (2%)
  matrix products  4.24 us (2%)
  local copies, waits for them, and re-layouts  3.85 us (2%)
    pallas_call x1, Pallas kernels, experts(): pl.pallas_call(expert_kernel, out_shape=jax.ShapeDtypeStruct((high.shape[...  149 us
    reduce_scatter x1, waiting for transfers between devices, local(): lax.psum_scatter(jnp.einsum('th,hd->dt', context, out_weight, preferred_e...  44.8 us
    psum x1, blocking collectives, local(): squares = lax.psum(jnp.sum(attended * attended, axis=1), 'tensor')  14.6 us
  transfers between devices with their start and end apart: 1, of which 1 were waited for; matrix products, arithmetic and copies ran while one was open for 1% of the time, Pallas kernels for 0%

profile of v2, /device:TPU:1, one launch (start us, length us, event | category | flops | bytes accessed | tf_op | source)
XLA Modules:
  0.0 236.7 jit_solution(11023933187766682013)
XLA Ops:
  7.2 0.0 copy-start
  7.2 0.0 copy-start.3
  7.2 0.0 copy-start.2
  7.2 0.0 copy-start.1
  7.2 0.0 reduce-scatter.2.cloned.1.call-start
  7.3 1.5 copy-done
  8.8 2.6 %fusion.28 = f32[2048,128]{1,0:T(8,128)} fusion(bf16[512,2048]{1,0:T(8,128)(2,1)S(1)} %copy-done, bf16[128,512]{1,0:T(8,128)(2,1)} %param.9), kind=kOutput, calls=%fused_computation.51 | convolution fusion | flops 268435456 | bytes 3276800 | tf_op jit(solution)/shard_map/th,hd->dt/dot_general | solution.py:281
  11.4 0.0 reduce-scatter.2.cloned.1.call-update
  11.5 0.0 copy-done.3
  11.5 0.0 copy-done.2
  11.6 0.1 fusion.3
  11.8 0.0 copy-done.1
  11.8 0.1 copy.15
  11.9 0.8 fusion.6
  12.7 1.2 fusion
  13.9 1.1 fusion.1.high_ref
  15.0 44.8 %reduce-scatter.2.cloned.1.call-done = f32[256,128]{1,0:T(8,128)} async-done(((f32[2048,128]{1,0:T(8,128)}), f32[256,128]{1,0:T(8,128)}) %reduce-scatter.2.cloned.1.call-update) | async-done | bytes 131088 | tf_op jit(solution)/shard_map/reduce_scatter | solution.py:280
  59.8 1.0 multiply_reduce_fusion
  60.7 14.6 %psum.7 = f32[128]{0:T(128)S(1)} all-reduce(f32[128]{0:T(128)S(1)} %get-tuple-element.8), channel_id=1, replica_groups=mesh['dp'=64,'tensor'=8] {'tensor'}, use_global_device_ids=true, to_apply=%region_5.6 | all-reduce | flops 128 | bytes 1024 | tf_op jit(solution)/shard_map/psum | solution.py:309
  75.3 0.8 copy.16
  76.1 0.7 fusion.4
  76.7 2.3 fusion.2.x_ref
  79.1 149.3 %shard_map.104 = bf16[128,256]{1,0:T(8,128)(2,1)} custom-call(bf16[3072,128]{1,0:T(8,128)(2,1)} %fusion.2.x_ref, bf16[128,3072]{1,0:T(8,128)(2,1)} %fusion.1.high_ref, bf16[128,3072]{1,0:T(8,128)(2,1)} %get-tuple-element.6.low_ref, bf16[192,2048]{1,0:T(8,128)(2,1)} %bitcast.9, bf16[192,2048]{1,0:T(8,128)(2,1)} %bitcast.10, bf16[1536,256]{1,0:T(8,128)(2,1)} %bitcast.11), custom_call_target="tpu_custom_call" | custom-call | tf_op jit(solution)/shard_map/pallas_call | solution.py:250
  228.4 1.5 copy.20
  (11 shorter events, 0.2 us)
Async XLA Ops:
  7.2 1.6 copy-start
  7.2 4.3 %copy-start.3 = (f32[128,8]{0,1:T(8,128)S(1)}, f32[128,8]{0,1:T(8,128)}, u32[]{:S(2)}) copy-start(f32[128,8]{0,1:T(8,128)} %param.14) | copy-start | bytes 12292
  7.2 4.3 %copy-start.2 = (s32[128,8]{0,1:T(8,128)S(1)}, s32[128,8]{0,1:T(8,128)}, u32[]{:S(2)}) copy-start(s32[128,8]{0,1:T(8,128)} %param.13) | copy-start | bytes 12292
  7.2 4.6 %copy-start.1 = (f32[128,256]{1,0:T(8,128)S(1)}, f32[128,256]{1,0:T(8,128)}, u32[]{:S(2)}) copy-start(f32[128,256]{1,0:T(8,128)} %param.11) | copy-start | bytes 393220
  7.2 52.6 %reduce-scatter.2.cloned.1.call-start = ((), (), s32[]{:S(2)}) async-start(), calls=%async_computation.1 | async-start | bytes 1179648 | tf_op jit(solution)/shard_map/reduce_scatter | solution.py:280
  13.9 62.2 %copy-start.4 = (f32[256]{0:T(256)S(1)}, f32[256]{0:T(256)}, u32[]{:S(2)}) copy-start(f32[256]{0:T(256)} %param.12) | copy-start | bytes 3076
Sparse Core Ops, SparseCore 0:
  11.5 48.1 reduce-scatter.1

commit v3 on v2

--- a/solution.py
+++ b/solution.py
@@ -79,14 +79,17 @@
     return z * 4 + lax.rem(lax.rem(dp // 2, 2) + a, 2) * 2 + lax.rem(lax.rem(dp, 2) + b, 2)
 
 
-def expert_kernel(
-    x_ref, high_ref, low_ref, gate_ref, up_ref, down_ref, out_ref,
-    xg, ag, wlo, whi, wd1, wd2, ob, ret, own_sem, d_send, d_recv, r_send, r_recv,
+def block_kernel(
+    context_ref, proj_ref, residual_ref, gain_ref, ids_ref, gates_ref, gate_ref, up_ref, down_ref,
+    attended_ref, out_ref,
+    ps, pr, sq, x_ref, place_ref, high_ref, low_ref, xg, ag, wlo, whi, wd1, wd2, ob, ret,
+    p_send, p_recv, s_send, s_recv, own_sem, d_send, d_recv, r_send, r_recv,
     x_send, x_recv, a_send, a_recv,
 ):
     slots = x_ref.shape[0]
     block = slots // DP
     row = block // 2
+    tokens, width = residual_ref.shape
     hidden = gate_ref.shape[0]
     rest = hidden - 128
     per = DP // CHUNKS
@@ -97,12 +100,35 @@
     me = lax.axis_index("dp")
 
     barrier = pltpu.get_barrier_semaphore()
-    for other in (partner, right, left):
+    for other in owners[1:]:
         pl.semaphore_signal(barrier, inc=1, device_id={"tensor": other}, device_id_type=MESH)
 
     @pl.loop(1, DP)
     def _(p):
         pl.semaphore_signal(barrier, inc=1, device_id={"dp": peer(p, 1)}, device_id_type=MESH)
+
+    def columns(slot):
+        return pl.ds(pl.multiple_of(owners[slot] * width, width), width)
+
+    def project(slot):
+        return jnp.dot(context_ref[...], proj_ref[:, columns(slot)], preferred_element_type=jnp.float32)
+
+    def to_all(src, dst, sends, recvs):
+        return {
+            k: pltpu.make_async_remote_copy(
+                src_ref=src(k), dst_ref=dst(k), send_sem=sends.at[k], recv_sem=recvs.at[k],
+                device_id={"tensor": owners[k]}, device_id_type=MESH,
+            )
+            for k in (7, 4, 5, 6, 2, 3, 1)
+        }
+
+    partials = to_all(lambda k: ps.at[k], lambda k: pr.at[k], p_send, p_recv)
+    for k in partials:
+        ps[k] = project(k).astype(jnp.bfloat16)
+    pl.semaphore_wait(barrier, 7 + DP - 1)
+    for k in partials:
+        partials[k].start()
+    total = residual_ref[...] + project(0)
 
     wlo[...] = jnp.zeros_like(wlo)
     whi[...] = jnp.zeros_like(whi)
@@ -118,7 +144,61 @@
         tail = down_ref[pl.ds(pl.multiple_of(base + 128, 64), rest), :]
         wd2[pl.ds(slot * 128, rest), 0:256] = tail
         wd2[pl.ds(slot * 128 + rest, rest), 256:512] = tail
-    pl.semaphore_wait(barrier, 3 + DP - 1)
+
+    gates = gates_ref[...]
+    weights = gates / jnp.sum(gates, axis=1, keepdims=True)
+    ids = ids_ref[...]
+    expert = lax.broadcasted_iota(jnp.int32, (tokens, DP), 1)
+    member = jnp.zeros((tokens, DP), jnp.float32)
+    weight = jnp.zeros((tokens, DP), jnp.float32)
+    for k in range(ids.shape[1]):
+        named = ids[:, k:k + 1] == expert
+        member = jnp.where(named, 1.0, member)
+        weight = jnp.where(named, weights[:, k:k + 1], weight)
+    before = jnp.where(
+        lax.broadcasted_iota(jnp.int32, (tokens, tokens), 1)
+        < lax.broadcasted_iota(jnp.int32, (tokens, tokens), 0),
+        1.0, 0.0,
+    ).astype(jnp.bfloat16)
+    rank = jnp.dot(before, member.astype(jnp.bfloat16), preferred_element_type=jnp.float32)
+    rank = jnp.where(member > 0.5, rank, -1.0)
+    slot_at = lax.broadcasted_iota(jnp.int32, (DP, slots), 1)
+    start = lax.broadcasted_iota(jnp.int32, (DP, slots), 0) * block
+    within = (slot_at >= start) & (slot_at < start + block)
+    spread = jnp.where(within, 1.0, 0.0).astype(jnp.bfloat16)
+    inside = jnp.sum(jnp.where(within, slot_at - start, 0).astype(jnp.float32), axis=0, keepdims=True)
+    inside = jnp.where(inside >= row, inside - row, inside)
+
+    def spread_out(v):
+        return jnp.dot(v.astype(jnp.bfloat16), spread, preferred_element_type=jnp.float32)
+
+    place = spread_out(rank) == inside
+    high = weight.astype(jnp.bfloat16).astype(jnp.float32)
+    high_ref[...] = jnp.where(place, spread_out(high), 0.0).astype(jnp.bfloat16)
+    low_ref[...] = jnp.where(place, spread_out(weight - high), 0.0).astype(jnp.bfloat16)
+    place_ref[...] = jnp.where(place, 1.0, 0.0).T.astype(jnp.bfloat16)
+
+    for k in reversed(list(partials)):
+        partials[k].wait_recv()
+        total = total + pr[k].astype(jnp.float32)
+    attended_ref[...] = total
+    squares = jnp.sum(total * total, axis=1, keepdims=True)
+    sq[0] = jnp.broadcast_to(squares, (tokens, 128)).T[0:8]
+    sums = to_all(lambda k: sq.at[0], lambda k: sq.at[k], s_send, s_recv)
+    for k in sums:
+        sums[k].start()
+    for k in sums:
+        sums[k].wait_recv()
+    squares = sq[0]
+    for k in range(1, 8):
+        squares = squares + sq[k]
+    squares = jnp.broadcast_to(squares[0:1], (128, tokens)).T[:, 0:1]
+    scaling = lax.rsqrt(squares / (width * 8) + epsilon)
+    normed = (total * scaling * gain_ref[...]).astype(jnp.bfloat16)
+
+    lower = lax.rem(lax.broadcasted_iota(jnp.int32, (slots, 128), 0), block) < row
+    rows = jnp.dot(place_ref[...], normed, preferred_element_type=jnp.float32)
+    x_ref[...] = jnp.where(lower, rows[:, 0:128], rows[:, 128:256]).astype(jnp.bfloat16)
 
     def rows_at(p):
         return pl.ds(pl.multiple_of(p * block, 16), block)
@@ -229,7 +309,6 @@
     wait_for(ret.at[others], r_recv)
 
     back = ret[...]
-    lower = lax.rem(lax.broadcasted_iota(jnp.int32, (slots, 128), 0), block) < row
     zero = jnp.zeros_like(back)
     back = jnp.concatenate([jnp.where(lower, back, zero), jnp.where(lower, zero, back)], axis=1)
     mixed = jnp.dot(high_ref[...], back, preferred_element_type=jnp.float32)
@@ -240,84 +319,54 @@
     wait_for(ob.at[others], r_send)
     for g in gx + ga:
         g.drain()
-
-
-def experts(x, high, low, gate, up, down):
-    slots = x.shape[0]
+    for c in [*partials.values(), *sums.values()]:
+        c.wait_send()
+
+
+def local(
+    context, out_weight, residual_in, norm_gain, expert_ids, expert_gates, w_gate, w_up, w_down
+):
+    tokens, width = residual_in.shape
+    slots = 3 * tokens * expert_ids.shape[1]
     packed = slots // 2 * 3 // 2
     vmem = pl.BlockSpec(memory_space=pltpu.VMEM)
     dma = pltpu.SemaphoreType.DMA
+    half = jnp.bfloat16
     return pl.pallas_call(
-        expert_kernel,
-        out_shape=jax.ShapeDtypeStruct((high.shape[0], 256), jnp.bfloat16),
-        in_specs=[vmem] * 6,
-        out_specs=vmem,
+        block_kernel,
+        out_shape=(
+            jax.ShapeDtypeStruct((tokens, width), jnp.float32),
+            jax.ShapeDtypeStruct((tokens, width), half),
+        ),
+        in_specs=[vmem] * 9,
+        out_specs=(vmem, vmem),
         scratch_shapes=[
-            pltpu.VMEM((slots, 8 * 128), jnp.bfloat16),
-            pltpu.VMEM((packed, 8 * 128), jnp.bfloat16),
-            pltpu.VMEM((512, 8 * 128), jnp.bfloat16),
-            pltpu.VMEM((512, 8 * 128), jnp.bfloat16),
-            pltpu.VMEM((8 * 128, 256), jnp.bfloat16),
-            pltpu.VMEM((8 * 128, 512), jnp.bfloat16),
-            pltpu.VMEM((slots, 128), jnp.bfloat16),
-            pltpu.VMEM((slots, 128), jnp.bfloat16),
+            pltpu.VMEM((8, tokens, width), half),
+            pltpu.VMEM((8, tokens, width), half),
+            pltpu.VMEM((8, 8, 128), jnp.float32),
+            pltpu.VMEM((slots, 128), half),
+            pltpu.VMEM((slots, tokens), half),
+            pltpu.VMEM((tokens, slots), half),
+            pltpu.VMEM((tokens, slots), half),
+            pltpu.VMEM((slots, 8 * 128), half),
+            pltpu.VMEM((packed, 8 * 128), half),
+            pltpu.VMEM((512, 8 * 128), half),
+            pltpu.VMEM((512, 8 * 128), half),
+            pltpu.VMEM((8 * 128, 256), half),
+            pltpu.VMEM((8 * 128, 512), half),
+            pltpu.VMEM((slots, 128), half),
+            pltpu.VMEM((slots, 128), half),
+            dma((8,)), dma((8,)), dma((8,)), dma((8,)),
             dma((2,)), dma, dma((CHUNKS,)), dma, dma,
             dma((CHUNKS, 8)), dma((CHUNKS, 8)), dma((CHUNKS, 8)), dma((CHUNKS, 8)),
         ],
         compiler_params=pltpu.CompilerParams(
-            collective_id=0, has_side_effects=True, vmem_limit_bytes=56 * 1024 * 1024
+            collective_id=0, has_side_effects=True, vmem_limit_bytes=60 * 1024 * 1024
         ),
-    )(x, high, low, gate, up, down)
-
-
-def local(
-    context, out_weight, residual_in, norm_gain, expert_ids, expert_gates, w_gate, w_up, w_down
-):
-    num_tokens, width_local = residual_in.shape
-    top_count = expert_ids.shape[1]
-    num_experts = w_gate.shape[0] * lax.axis_size("dp")
-    capacity = max(2, 3 * num_tokens * top_count // (2 * num_experts))
-    summed_proj = lax.psum_scatter(
-        jnp.einsum("th,hd->dt", context, out_weight, preferred_element_type=jnp.float32),
-        "tensor",
-        scatter_dimension=0,
-        tiled=True,
+    )(
+        context, out_weight, residual_in, norm_gain[None, :], expert_ids, expert_gates,
+        w_gate[0], w_up[0], w_down[0],
     )
-    weights = expert_gates / jnp.sum(expert_gates, axis=1, keepdims=True)
-    named = expert_ids[:, :, None] == jnp.arange(num_experts, dtype=jnp.int32)[None, None, :]
-    member = jnp.any(named, axis=1)
-    weight = jnp.sum(jnp.where(named, weights[:, :, None], 0.0), axis=1)
-    order = jnp.arange(num_tokens, dtype=jnp.int32)
-    before = (order[None, :] < order[:, None]).astype(jnp.bfloat16)
-    rank = jnp.dot(before, member.astype(jnp.bfloat16), preferred_element_type=jnp.float32)
-    rank = jnp.where(member, rank, -1.0).astype(jnp.bfloat16)
-    block = 2 * capacity
-    slot = jnp.arange(num_experts * block, dtype=jnp.int32)
-    spread = (slot[None, :] // block == jnp.arange(num_experts, dtype=jnp.int32)[:, None]).astype(
-        jnp.bfloat16
-    )
-    high = lax.reduce_precision(weight, 8, 7)
-    low = weight - high
-    stacked = jnp.concatenate([rank, high.astype(jnp.bfloat16), low.astype(jnp.bfloat16)], axis=0)
-    wide = jnp.dot(stacked, spread, preferred_element_type=jnp.float32)
-    place = wide[:num_tokens] == (slot % capacity).astype(jnp.float32)[None, :]
-    mix_high = jnp.where(place, wide[num_tokens:2 * num_tokens], 0.0).astype(jnp.bfloat16)
-    mix_low = jnp.where(place, wide[2 * num_tokens:], 0.0).astype(jnp.bfloat16)
-    place = place.astype(jnp.bfloat16)
-
-    attended = residual_in + summed_proj.T
-    squares = lax.psum(jnp.sum(attended * attended, axis=1), "tensor")
-    full_width = width_local * lax.axis_size("tensor")
-    scaling = lax.rsqrt(squares / full_width + epsilon)
-    normed = (attended * scaling[:, None] * norm_gain).astype(jnp.bfloat16)
-
-    outgoing = lax.dot_general(
-        place, normed, (((0,), (0,)), ((), ())), preferred_element_type=jnp.float32
-    )
-    lower = (slot % block < capacity)[:, None]
-    outgoing = jnp.where(lower, outgoing[:, :128], outgoing[:, 128:]).astype(jnp.bfloat16)
-    mixed = experts(outgoing, mix_high, mix_low, w_gate[0], w_up[0], w_down[0])
-    return (attended, mixed)
 
 
 def solution(mesh):

time: 240 us -> 173 us (0.72)
  the two profiles are of different devices: /device:TPU:1 before, /device:TPU:97 now
where the time goes in v3:
time: 173 us; the launch traced here: 172 us
  Pallas kernels  166 us (96%)
  local copies, waits for them, and re-layouts  5.87 us (3%)
    pallas_call x1, Pallas kernels, local(): pl.pallas_call(block_kernel, out_shape=(jax.ShapeDtypeStruct((tokens, wid...  166 us
    unnamed x4, local copies, waits for them, and re-layouts  5.87 us

profile of v3, /device:TPU:97, one launch (start us, length us, event | category | flops | bytes accessed | tf_op | source)
XLA Modules:
  0.0 172.4 jit_solution(12732250376225118921)
XLA Ops:
  0.6 1.4 copy.11.ids_ref
  2.0 1.4 copy.12.gates_ref
  3.5 165.8 %shard_map.104 = (f32[128,256]{1,0:T(8,128)}, bf16[128,256]{1,0:T(8,128)(2,1)}) custom-call(bf16[128,512]{1,0:T(8,128)(2,1)} %context_ref.1, bf16[512,2048]{1,0:T(8,128)(2,1)} %proj_ref.1, f32[128,256]{1,0:T(8,128)} %residual_ref.1, f32[1,256]{1,0:T(1,128)} %bitcast.7, s32[128,8]{1,0:T(8,128)} %copy.11.ids_ref, f32[128,8]{1,0:T(8,128)} %copy.12.gates_ref, ...), custom_call_target="tpu_custom_call" | custom-call | tf_op jit(solution)/shard_map/pallas_call | solution.py:335
  169.3 1.6 copy.15
  170.9 1.5 copy.16

commit v4 on v3

--- a/solution.py
+++ b/solution.py
@@ -10,7 +10,7 @@
 epsilon = 1e-06
 MESH = pl.DeviceIdType.MESH
 NX, NY, NZ, DP = 4, 2, 16, 64
-CHUNKS = 4
+CHUNKS = 8
 
 
 def neighbours():
@@ -70,13 +70,20 @@
             c.wait_send()
 
 
-def peer(p, sign):
+ORDER = (0, 1, 4, 12, 8, 9, 7, 10, 6, 11, 5, 13, 3, 14, 2, 15)
+
+
+def peer(dz, q):
     dp = lax.axis_index("dp")
-    i, a, b = p // 4, lax.rem(p // 2, 2), lax.rem(p, 2)
-    odd = lax.rem(i, 2)
-    dz = odd * ((i + 1) // 2) + (1 - odd) * lax.rem(NZ - i // 2, NZ)
-    z = lax.rem(dp // 4 + NZ + sign * dz, NZ)
-    return z * 4 + lax.rem(lax.rem(dp // 2, 2) + a, 2) * 2 + lax.rem(lax.rem(dp, 2) + b, 2)
+    z = lax.rem(dp // 4 + dz, NZ)
+    return z * 4 + lax.rem(lax.rem(dp // 2, 2) + q // 2, 2) * 2 + lax.rem(lax.rem(dp, 2) + lax.rem(q, 2), 2)
+
+
+def each_peer(body, first=0, last=NZ):
+    for i in range(first, last):
+        @pl.loop(1 if i == 0 else 0, 4)
+        def _(q):
+            body(4 * i + q, peer(ORDER[i], q), peer(NZ - ORDER[i], q))
 
 
 def block_kernel(
@@ -105,7 +112,7 @@
 
     @pl.loop(1, DP)
     def _(p):
-        pl.semaphore_signal(barrier, inc=1, device_id={"dp": peer(p, 1)}, device_id_type=MESH)
+        pl.semaphore_signal(barrier, inc=1, device_id={"dp": lax.rem(me + p, DP)}, device_id_type=MESH)
 
     def columns(slot):
         return pl.ds(pl.multiple_of(owners[slot] * width, width), width)
@@ -130,25 +137,10 @@
         partials[k].start()
     total = residual_ref[...] + project(0)
 
-    wlo[...] = jnp.zeros_like(wlo)
-    whi[...] = jnp.zeros_like(whi)
-    wd2[...] = jnp.zeros_like(wd2)
-    for slot, owner in enumerate(owners):
-        here = pl.ds(slot * 128, 128)
-        for part, w in enumerate((wlo, whi)):
-            cols = pl.ds(pl.multiple_of(owner * 256 + part * 128, 128), 128)
-            w[0:hidden, here] = gate_ref[:, cols]
-            w[256:256 + hidden, here] = up_ref[:, cols]
-        base = owner * hidden
-        wd1[here, :] = down_ref[pl.ds(pl.multiple_of(base, 64), 128), :]
-        tail = down_ref[pl.ds(pl.multiple_of(base + 128, 64), rest), :]
-        wd2[pl.ds(slot * 128, rest), 0:256] = tail
-        wd2[pl.ds(slot * 128 + rest, rest), 256:512] = tail
-
     gates = gates_ref[...]
-    weights = gates / jnp.sum(gates, axis=1, keepdims=True)
-    ids = ids_ref[...]
-    expert = lax.broadcasted_iota(jnp.int32, (tokens, DP), 1)
+    weights = (gates / jnp.sum(gates, axis=0, keepdims=True)).T
+    ids = ids_ref[...].astype(jnp.float32).T
+    expert = lax.broadcasted_iota(jnp.int32, (tokens, DP), 1).astype(jnp.float32)
     member = jnp.zeros((tokens, DP), jnp.float32)
     weight = jnp.zeros((tokens, DP), jnp.float32)
     for k in range(ids.shape[1]):
@@ -173,10 +165,15 @@
         return jnp.dot(v.astype(jnp.bfloat16), spread, preferred_element_type=jnp.float32)
 
     place = spread_out(rank) == inside
-    high = weight.astype(jnp.bfloat16).astype(jnp.float32)
-    high_ref[...] = jnp.where(place, spread_out(high), 0.0).astype(jnp.bfloat16)
-    low_ref[...] = jnp.where(place, spread_out(weight - high), 0.0).astype(jnp.bfloat16)
-    place_ref[...] = jnp.where(place, 1.0, 0.0).T.astype(jnp.bfloat16)
+    place = jnp.where(place, 1.0, 0.0)
+    high_ref[...] = place.astype(jnp.bfloat16)
+    place_ref[...] = place.T.astype(jnp.bfloat16)
+
+    def mix_matrices():
+        place = high_ref[...].astype(jnp.float32)
+        high = weight.astype(jnp.bfloat16).astype(jnp.float32)
+        high_ref[...] = (place * spread_out(high)).astype(jnp.bfloat16)
+        low_ref[...] = (place * spread_out(weight - high)).astype(jnp.bfloat16)
 
     for k in reversed(list(partials)):
         partials[k].wait_recv()
@@ -203,24 +200,19 @@
     def rows_at(p):
         return pl.ds(pl.multiple_of(p * block, 16), block)
 
-    def send(p):
-        to = peer(p, -1)
-        return pltpu.make_async_remote_copy(
+    def send(p, _, to):
+        pltpu.make_async_remote_copy(
             src_ref=x_ref.at[rows_at(to)], dst_ref=xg.at[rows_at(p), pl.ds(0, 128)],
             send_sem=d_send, recv_sem=d_recv.at[p // per], device_id={"dp": to}, device_id_type=MESH,
-        )
-
-    def give_back(p):
-        to = peer(p, 1)
-        return pltpu.make_async_remote_copy(
+        ).start()
+
+    def give_back(p, to, _):
+        pltpu.make_async_remote_copy(
             src_ref=ob.at[rows_at(p)], dst_ref=ret.at[rows_at(me)],
             send_sem=r_send, recv_sem=r_recv, device_id={"dp": to}, device_id_type=MESH,
-        )
-
-    @pl.loop(1, DP)
-    def _(p):
-        send(p).start()
-
+        ).start()
+
+    each_peer(send)
     own = pltpu.make_async_copy(x_ref.at[rows_at(me)], xg.at[pl.ds(0, block), pl.ds(0, 128)], own_sem.at[0])
     own.start()
     own_back = pltpu.make_async_copy(ob.at[pl.ds(0, block)], ret.at[rows_at(me)], own_sem.at[1])
@@ -280,9 +272,23 @@
         if c == 0:
             own_back.start()
 
-        @pl.loop(max(1, c * per), (c + 1) * per)
-        def _(p):
-            give_back(p).start()
+        each_peer(give_back, c * per // 4, (c + 1) * per // 4)
+
+    def arrange_weights():
+        wlo[...] = jnp.zeros_like(wlo)
+        whi[...] = jnp.zeros_like(whi)
+        wd2[...] = jnp.zeros_like(wd2)
+        for slot, owner in enumerate(owners):
+            here = pl.ds(slot * 128, 128)
+            for part, w in enumerate((wlo, whi)):
+                cols = pl.ds(pl.multiple_of(owner * 256 + part * 128, 128), 128)
+                w[0:hidden, here] = gate_ref[:, cols]
+                w[256:256 + hidden, here] = up_ref[:, cols]
+            base = owner * hidden
+            wd1[here, :] = down_ref[pl.ds(pl.multiple_of(base, 64), 128), :]
+            tail = down_ref[pl.ds(pl.multiple_of(base + 128, 64), rest), :]
+            wd2[pl.ds(slot * 128, rest), 0:256] = tail
+            wd2[pl.ds(slot * 128 + rest, rest), 256:512] = tail
 
     for step in range(CHUNKS + 6):
         at = lambda lag: step - lag if 0 <= step - lag < CHUNKS else None
@@ -291,6 +297,10 @@
             gx[at(0)].start()
         if at(1) is not None:
             gx[at(1)].relay()
+        if step == 1:
+            arrange_weights()
+        if step == 6:
+            mix_matrices()
         if at(2) is not None:
             gx[at(2)].cross()
         if at(3) is not None:
@@ -364,7 +374,7 @@
             collective_id=0, has_side_effects=True, vmem_limit_bytes=60 * 1024 * 1024
         ),
     )(
-        context, out_weight, residual_in, norm_gain[None, :], expert_ids, expert_gates,
+        context, out_weight, residual_in, norm_gain[None, :], expert_ids.T, expert_gates.T,
         w_gate[0], w_up[0], w_down[0],
     )
 

time: 173 us -> 153 us (0.88)
  the two profiles are of different devices: /device:TPU:97 before, /device:TPU:1 now
where the time goes in v4:
time: 153 us
  Pallas kernels  150 us (98%)
  local copies, waits for them, and re-layouts  3.04 us (2%)
    pallas_call x1, Pallas kernels, local(): pl.pallas_call(block_kernel, out_shape=(jax.ShapeDtypeStruct((tokens, wid...  150 us

profile of v4, /device:TPU:1, one launch (start us, length us, event | category | flops | bytes accessed | tf_op | source)
XLA Modules:
  0.0 153.2 jit_solution(9290827210044341479)
XLA Ops:
  0.6 149.5 %shard_map.104 = (f32[128,256]{1,0:T(8,128)}, bf16[128,256]{1,0:T(8,128)(2,1)}) custom-call(bf16[128,512]{1,0:T(8,128)(2,1)} %context_ref.1, bf16[512,2048]{1,0:T(8,128)(2,1)} %proj_ref.1, f32[128,256]{1,0:T(8,128)} %residual_ref.1, f32[1,256]{1,0:T(1,128)} %bitcast.11, s32[8,128]{1,0:T(8,128)} %bitcast.9, f32[8,128]{1,0:T(8,128)} %bitcast.10, ...), custom_call_target="tpu_custom_call" | custom-call | tf_op jit(solution)/shard_map/pallas_call | solution.py:345
  150.2 1.6 %copy.13 = f32[128,256]{1,0:T(8,128)} copy(f32[128,256]{1,0:T(8,128)} %get-tuple-element.4) | data formatting | bytes 262144
  151.7 1.5 copy.14
